TPU v7x, 512 devices: a whole 4x8x8 slice. The times are simulated.
512 devices in a mesh: fsdp: 32 (over y, x_hi, core), tensor: 16 (over x_lo, z).
Axes of the slice: x: 4 (x_hi: 2, x_lo: 2; x = x_hi * 2 + x_lo), y: 8, z: 8, core: 2. Of those that a mesh axis runs over, the one named last changes fastest.
Arguments:
- out_grad: bfloat16 [4096, 8192], P(('fsdp', 'tensor')), may hold values from -24 to 24
- live_rows: int32 [512], P(('fsdp', 'tensor')), may hold values from 1 to 8, as said below
- gate_pre: bfloat16 [4096, 12288], P('fsdp', 'tensor'), may hold values from -8 to 8
- up_pre: bfloat16 [4096, 12288], P('fsdp', 'tensor'), may hold values from -6 to 6
- down_weight: bfloat16 [12288, 8192], P('tensor', 'fsdp'), may hold values from -0.15625 to 0.15625
- tile_mask: int32 [96, 64], P('tensor'), may hold values from 0 to 1, as said below
Outputs:
- d_gate: bfloat16 [4096, 12288], P('fsdp', 'tensor')
- d_up: bfloat16 [4096, 12288], P('fsdp', 'tensor')
- d_weight: bfloat16 [12288, 8192], P('tensor', 'fsdp')
Inputs may be any that keep to these rules, and one draw needn't show every extreme that they name: `tile_mask`: each device's shard of 6 x 2 tiles holds 1 to 4 kept tiles; in every draw the shards of some tensor index all hold exactly 4, and every tensor index has a shard holding 4. `live_rows`: some device has all 8 rows live in every draw.
All inputs are finite; a program needn't handle non-finite values.
Results may differ from a plain program's by a relative error of at most 0.015.
Values may be sent and summed in bfloat16 or wider, within the bound.
No kernel may reach another device: no remote copies, remote signals or barrier semaphores. Data moves between devices by JAX's collectives and lax.ppermute only.
A program may use at most 64 MiB of HBM per device.

v0:
```python
import math
import jax
import jax.numpy as jnp
from jax import lax
from jax.sharding import PartitionSpec as P

BLK = 128
CAP = 4


def split_count(slot_count):
    group_size = CAP * math.gcd(slot_count // CAP, 8)
    return (group_size, slot_count // group_size)


def per_device(out_grad, live_rows, gate_pre, up_pre, down_weight, tile_mask):
    fsdp_count = lax.axis_size("fsdp")
    fsdp_index = lax.axis_index("fsdp")
    tok_rows = out_grad.shape[0]
    row_blocks = tile_mask.shape[0]
    col_blocks = down_weight.shape[1] // BLK
    local_count = row_blocks * col_blocks
    live_mask = jnp.arange(tok_rows)[:, None] < live_rows[0]
    masked_grad = jnp.where(live_mask, out_grad, jnp.zeros_like(out_grad))
    grad_panel = lax.all_gather(masked_grad, "tensor", axis=0, tiled=True)
    rows_all = grad_panel.shape[0]
    panel_tiles = grad_panel.reshape(rows_all, fsdp_count * col_blocks, BLK)
    shard_masks = (
        tile_mask.reshape(row_blocks, fsdp_count, col_blocks)
        .transpose(1, 0, 2)
        .reshape(fsdp_count, local_count)
    )
    position = jnp.cumsum(shard_masks, axis=1) - 1
    chosen = (shard_masks[:, None, :] == 1) & (
        position[:, None, :] == jnp.arange(CAP)[None, :, None]
    )
    chosen_int = chosen.astype(jnp.int32)
    block_id = jnp.sum(chosen_int * jnp.arange(local_count)[None, None, :], axis=2)
    occupied = jnp.sum(chosen_int, axis=2)
    tile_row = (block_id // col_blocks).reshape(-1)
    tile_col = (jnp.arange(fsdp_count)[:, None] * col_blocks + block_id % col_blocks).reshape(-1)
    tile_live = occupied.reshape(-1).astype(jnp.float32)
    own_choice = lax.dynamic_index_in_dim(chosen_int, fsdp_index, 0, keepdims=False)
    local_tiles = (
        down_weight.reshape(row_blocks, BLK, col_blocks, BLK)
        .transpose(0, 2, 1, 3)
        .reshape(local_count, BLK, BLK)
    )
    packed = jnp.einsum(
        "sb,bij->sij",
        own_choice.astype(jnp.bfloat16),
        local_tiles,
        preferred_element_type=jnp.float32,
    ).astype(jnp.bfloat16)
    gate_value = gate_pre.astype(jnp.float32)
    up_value = up_pre.astype(jnp.float32)
    sigmoid_gate = jax.nn.sigmoid(gate_value)
    hidden = (gate_value * sigmoid_gate * up_value).astype(jnp.bfloat16)
    hidden_tiles = hidden.reshape(rows_all, row_blocks, BLK)
    grad_scale = 1.0 / math.sqrt(rows_all * fsdp_count)
    row_ids = jnp.arange(row_blocks)
    start_sum = jnp.zeros((rows_all, row_blocks, BLK), jnp.float32)
    running_sum = start_sum
    shard_piece = lax.all_gather(packed, "fsdp", axis=0, tiled=True)
    slot_count = shard_piece.shape[0]
    group_size, group_count = split_count(slot_count)
    rows_part = tile_row.reshape(group_count, group_size)
    cols_part = tile_col.reshape(group_count, group_size)

    def add_one_turn(running, parts):
        tile_block, rows_sel, cols_sel = parts
        inputs = jnp.take(panel_tiles, cols_sel, axis=1)
        product = jnp.einsum("rsj,sij->rsi", inputs, tile_block, preferred_element_type=jnp.float32)
        placement = (rows_sel[:, None] == row_ids[None, :]).astype(jnp.float32)
        return (
            running
            + jnp.einsum("rsi,sb->rbi", product, placement, precision=lax.Precision.HIGHEST),
            None,
        )

    running_sum, _ = lax.scan(
        add_one_turn,
        running_sum,
        (shard_piece.reshape(group_count, group_size, BLK, BLK), rows_part, cols_part),
    )
    d_hidden = running_sum.reshape(rows_all, row_blocks * BLK)
    d_up = (d_hidden * gate_value * sigmoid_gate).astype(jnp.bfloat16)
    d_gate = (
        d_hidden * up_value * sigmoid_gate * (1.0 + gate_value * (1.0 - sigmoid_gate))
    ).astype(jnp.bfloat16)
    slot_count = fsdp_count * CAP
    group_size, group_count = split_count(slot_count)
    rows_part = tile_row.reshape(group_count, group_size)
    cols_part = tile_col.reshape(group_count, group_size)
    live_part = tile_live.reshape(group_count, group_size)

    def slot_one_turn(parts):
        rows_sel, cols_sel, live_sel = parts
        left_tiles = jnp.take(hidden_tiles, rows_sel, axis=1)
        right_tiles = jnp.take(panel_tiles, cols_sel, axis=1)
        slot_term = jnp.einsum(
            "rsi,rsj->sij", left_tiles, right_tiles, preferred_element_type=jnp.float32
        )
        return slot_term * (grad_scale * live_sel)[:, None, None]

    own_sums = lax.psum_scatter(
        lax.map(slot_one_turn, (rows_part, cols_part, live_part))
        .reshape(slot_count, BLK, BLK)
        .astype(jnp.bfloat16),
        "fsdp",
        scatter_dimension=0,
        tiled=True,
    ).astype(jnp.float32)
    dense_tiles = jnp.einsum(
        "sb,sij->bij", own_choice.astype(jnp.float32), own_sums, precision=lax.Precision.HIGHEST
    )
    d_weight = dense_tiles.reshape(row_blocks, col_blocks, BLK, BLK).transpose(0, 2, 1, 3)
    d_weight = d_weight.reshape(row_blocks * BLK, col_blocks * BLK).astype(jnp.bfloat16)
    return (d_gate, d_up, d_weight)


def solution(mesh):
    return jax.shard_map(
        per_device,
        mesh=mesh,
        in_specs=(
            P(("fsdp", "tensor"), None),
            P(("fsdp", "tensor")),
            P("fsdp", "tensor"),
            P("fsdp", "tensor"),
            P("tensor", "fsdp"),
            P("tensor", None),
        ),
        out_specs=(P("fsdp", "tensor"), P("fsdp", "tensor"), P("tensor", "fsdp")),
        check_vma=False,
    )
```

profile of v0, /device:TPU:16, one launch (start us, length us, event | category | flops | bytes accessed | tf_op | source)
XLA Modules:
  0.0 382.2 jit_solution(10613646936179450982)
XLA Ops:
  8.0 1.6 broadcast_select_fusion
  9.7 0.8 copy.57
  10.8 1.1 reshape.120
  12.0 0.3 convolution_convert_fusion.1
  12.3 0.7 copy.63
  13.3 1.2 fusion.49
  15.0 74.8 %all-gather.5.cloned.1.call-done = bf16[128,8192]{1,0:T(8,128)(2,1)} async-done(((bf16[8,8192]{1,0:T(8,128)(2,1)}), bf16[128,8192]{1,0:T(8,128)(2,1)}) %all-gather.5.cloned.1.call-update) | async-done | bytes 2097168 | tf_op jit(solution)/shard_map/all_gather | solution.py:25
  89.8 3.2 copy.64
  93.0 2.9 copy.65
  95.9 84.9 %all-gather.3.cloned.1.call-done = bf16[128,128,128]{2,1,0:T(8,128)(2,1)} async-done(((bf16[4,128,128]{2,1,0:T(8,128)(2,1)}), bf16[128,128,128]{2,1,0:T(8,128)(2,1)}) %all-gather.3.cloned.1.call-update) | async-done | bytes 4194320 | tf_op jit(solution)/shard_map/all_gather | solution.py:64
  180.9 36.9 %while.22 = (s32[]{:T(128)}, f32[128,6,128]{2,1,0:T(8,128)S(1)}, s32[4,32]{1,0:T(4,128)S(1)}, bf16[4,32,128,128]{3,2,1,0:T(8,128)(2,1)}, s32[4,32]{1,0:T(4,128)S...) while((s32[]{:T(128)}, f32[128,6,128]{2,1,0:T(8,128)S(1)}, s32[4,32]{1,0:T(4,128)S(1)}, ...), condition=%wide.region_3.5_spmd.clone, body=%wide.region_2.4_spmd.clone.sunk | while | flops 172688768 | bytes 13374515 | solution.py:81
  180.9 2.3 gather_fusion.2
  183.3 3.5 convolution_bitcast_fusion.3
  186.8 2.4 copy.93
  189.1 0.9 fusion.71
  190.2 2.3 gather_fusion.2
  192.5 3.5 convolution_bitcast_fusion.3
  196.0 2.4 copy.93
  198.4 0.9 fusion.71
  199.4 2.3 gather_fusion.2
  201.7 3.5 convolution_bitcast_fusion.3
  205.2 2.4 copy.93
  207.6 0.9 fusion.71
  208.6 2.3 gather_fusion.2
  211.0 3.5 convolution_bitcast_fusion.3
  214.5 2.4 copy.93
  216.9 0.9 fusion.71
  217.8 0.2 copy.66
  218.0 0.3 fusion.39
  218.5 19.4 %while.21 = (s32[]{:T(128)}, bf16[4,32,128,128]{3,2,1,0:T(8,128)(2,1)}, s32[4,32]{1,0:T(4,128)S(1)}, bf16[128,6,128]{2,0,1:T(8,128)(2,1)S(1)}, s32[4,32]{1,0:T(4...) while((s32[]{:T(128)}, bf16[4,32,128,128]{3,2,1,0:T(8,128)(2,1)}, ...), condition=%wide.region_6.8_spmd, body=%wide.region_5.7_spmd.sunk | while | flops 135793152 | bytes 8398573 | solution.py:107
  218.6 0.7 gather_fusion.1
  219.3 2.3 gather_fusion
  221.7 1.6 bitcast_dynamic-update-slice_fusion.2
  223.4 0.7 gather_fusion.1
  224.1 2.3 gather_fusion
  226.5 1.7 bitcast_dynamic-update-slice_fusion.2
  228.2 0.7 gather_fusion.1
  229.0 2.3 gather_fusion
  231.3 1.7 bitcast_dynamic-update-slice_fusion.2
  233.1 0.7 gather_fusion.1
  233.8 2.3 gather_fusion
  236.2 1.7 bitcast_dynamic-update-slice_fusion.2
  238.1 0.8 copy.76
  238.9 0.8 copy.75
  239.7 133.2 %reduce-scatter.2.cloned.1.call-done = bf16[4,128,128]{2,1,0:T(8,128)(2,1)} async-done(((bf16[128,128,128]{2,1,0:T(8,128)(2,1)}), bf16[4,128,128]{2,1,0:T(8,128)(2,1)}) %reduce-scatter.2.cloned.1.call-update) | async-done | bytes 131088 | tf_op jit(solution)/shard_map/reduce_scatter | solution.py:106
  372.9 1.5 fusion.28
  374.4 0.4 copy.74
  374.9 0.8 copy.91
  (67 shorter events, 1.9 us)
Async XLA Ops:
  7.2 7.4 %copy-start = (bf16[128,768]{1,0:T(8,128)(2,1)S(1)}, bf16[128,768]{1,0:T(8,128)(2,1)}, u32[]{:S(2)}) copy-start(bf16[128,768]{1,0:T(8,128)(2,1)} %param.14) | copy-start | bytes 589828
  7.2 7.6 %copy-start.1 = (bf16[128,768]{1,0:T(8,128)(2,1)S(1)}, bf16[128,768]{1,0:T(8,128)(2,1)}, u32[]{:S(2)}) copy-start(bf16[128,768]{1,0:T(8,128)(2,1)} %param.15) | copy-start | bytes 589828
  7.2 82.6 %all-gather.5.cloned.1.call-start = ((), (), s32[]{:S(2)}) async-start(), calls=%async_computation.2 | async-start | bytes 2228224 | tf_op jit(solution)/shard_map/all_gather | solution.py:25
  9.6 171.3 %all-gather.3.cloned.1.call-start = ((), (), s32[]{:S(2)}) async-start(), calls=%async_computation.1 | async-start | bytes 4325376 | tf_op jit(solution)/shard_map/all_gather | solution.py:64
  13.0 359.9 %reduce-scatter.2.cloned.1.call-start = ((), (), s32[]{:S(2)}) async-start(), calls=%async_computation.3 | async-start | bytes 4325376 | tf_op jit(solution)/shard_map/reduce_scatter | solution.py:106
Sparse Core Ops, SparseCore 0:
  10.6 79.0 all-gather.4
  93.7 87.1 all-gather.2
  238.0 134.8 reduce-scatter.1
where the time goes:
time: 383 us; the launch traced here: 382 us
  waiting for transfers between devices  293 us (77%)
  local copies, waits for them, and re-layouts  44.3 us (12%)
  matrix products  26.3 us (7%)
  between operations  14.6 us (4%)
    reduce_scatter x1, waiting for transfers between devices, per_device(): lax.psum_scatter(lax.map(slot_one_turn, (rows_part, cols_part, live_part)...  133 us
    all_gather x1, waiting for transfers between devices, per_device(): shard_piece = lax.all_gather(packed, 'fsdp', axis=0, tiled=True)  84.9 us
    all_gather x1, waiting for transfers between devices, per_device(): grad_panel = lax.all_gather(masked_grad, 'tensor', axis=0, tiled=True)  74.8 us
    dot_general x4, matrix products, add_one_turn(): jnp.einsum('rsj,sij->rsi', inputs, tile_block, preferred_element_type=jnp...  14 us
    transpose x4, local copies, waits for them, and re-layouts, add_one_turn(): jnp.einsum('rsj,sij->rsi', inputs, tile_block, preferred_element_type=jnp...  9.48 us
    gather x4, local copies, waits for them, and re-layouts, add_one_turn(): inputs = jnp.take(panel_tiles, cols_sel, axis=1)  9.36 us
    gather x4, local copies, waits for them, and re-layouts, slot_one_turn(): right_tiles = jnp.take(panel_tiles, cols_sel, axis=1)  9.36 us
  transfers between devices with their start and end apart: 3, of which 3 were waited for; matrix products, arithmetic and copies ran while one was open for 3% of the time, Pallas kernels for 0%

commit v1 on v0

--- a/solution.py
+++ b/solution.py
@@ -22,7 +22,9 @@
     local_count = row_blocks * col_blocks
     live_mask = jnp.arange(tok_rows)[:, None] < live_rows[0]
     masked_grad = jnp.where(live_mask, out_grad, jnp.zeros_like(out_grad))
-    grad_panel = lax.all_gather(masked_grad, "tensor", axis=0, tiled=True)
+    grad_panel = jnp.concatenate(
+        lax.all_to_all(jnp.stack([masked_grad] * lax.axis_size("tensor")), "tensor", 0, 0), axis=0
+    )
     rows_all = grad_panel.shape[0]
     panel_tiles = grad_panel.reshape(rows_all, fsdp_count * col_blocks, BLK)
     shard_masks = (

time: 383 us -> 313 us (0.82)
  waiting for transfers between devices: 293 us -> 214 us
  starting transfers between devices: 0.12 us -> 11.6 us
    all_gather x1 -> x0, waiting for transfers between devices: 74.8 us -> none  [per_device(): grad_panel = lax.all_gather(masked_grad, 'tensor', axis=0, tiled=True)]
    all_gather x1, waiting for transfers between devices: 84.9 us -> 34 us  [per_device(): shard_piece = lax.all_gather(packed, 'fsdp', axis=0, tiled=True)]
    all_to_all x0 -> x1, waiting for transfers between devices: none -> 46.8 us  [per_device(): lax.all_to_all(jnp.stack([masked_grad] * lax.axis_size('tensor')), 'tenso...]
    all_to_all x0 -> x1, starting transfers between devices: none -> 11.5 us  [per_device(): lax.all_to_all(jnp.stack([masked_grad] * lax.axis_size('tensor')), 'tenso...]
where the time goes in v1:
time: 313 us; the launch traced here: 312 us
  waiting for transfers between devices  214 us (68%)
  local copies, waits for them, and re-layouts  43.1 us (14%)
  matrix products  26.3 us (8%)
  between operations  14.9 us (5%)
  starting transfers between devices  11.6 us (4%)
    reduce_scatter x1, waiting for transfers between devices, per_device(): lax.psum_scatter(lax.map(slot_one_turn, (rows_part, cols_part, live_part)...  133 us
    all_to_all x1, waiting for transfers between devices, per_device(): lax.all_to_all(jnp.stack([masked_grad] * lax.axis_size('tensor')), 'tenso...  46.8 us
    all_gather x1, waiting for transfers between devices, per_device(): shard_piece = lax.all_gather(packed, 'fsdp', axis=0, tiled=True)  34 us
    dot_general x4, matrix products, add_one_turn(): jnp.einsum('rsj,sij->rsi', inputs, tile_block, preferred_element_type=jnp...  13.9 us
    all_to_all x1, starting transfers between devices, per_device(): lax.all_to_all(jnp.stack([masked_grad] * lax.axis_size('tensor')), 'tenso...  11.5 us
    transpose x4, local copies, waits for them, and re-layouts, add_one_turn(): jnp.einsum('rsj,sij->rsi', inputs, tile_block, preferred_element_type=jnp...  9.48 us
    gather x4, local copies, waits for them, and re-layouts, add_one_turn(): inputs = jnp.take(panel_tiles, cols_sel, axis=1)  9.36 us
    gather x4, local copies, waits for them, and re-layouts, slot_one_turn(): right_tiles = jnp.take(panel_tiles, cols_sel, axis=1)  9.36 us
  transfers between devices with their start and end apart: 3, of which 3 were waited for; matrix products, arithmetic and copies ran while one was open for 3% of the time, Pallas kernels for 0%

profile of v1, /device:TPU:16, one launch (start us, length us, event | category | flops | bytes accessed | tf_op | source)
XLA Modules:
  0.0 312.1 jit_solution(5391269633309313420)
XLA Ops:
  7.2 0.8 copy.56
  8.4 1.1 reshape.119
  9.6 0.3 convolution_convert_fusion.1
  9.9 0.7 copy.62
  11.4 1.6 stack.2
  12.9 11.5 %all-to-all-start = ((bf16[16,8,8192]{2,1,0:T(8,128)(2,1)}), bf16[16,8,8192]{2,1,0:T(8,128)(2,1)S(1)}, u32[]{:S(2)}, u32[]{:S(2)}) async-start(bf16[16,8,8192]{2,1,0:T(8,128)(2,1)} %stack.2), calls=%async_computation | async-start | bytes 4194304 | tf_op jit(solution)/shard_map/all_to_all | solution.py:26
  24.6 1.2 fusion.49
  26.3 46.8 %all-to-all-done = bf16[16,8,8192]{2,1,0:T(8,128)(2,1)S(1)} async-done(((bf16[16,8,8192]{2,1,0:T(8,128)(2,1)}), bf16[16,8,8192]{2,1,0:T(8,128)(2,1)S(1)}, u32[]{:S(2)}, u32[]{:S(2)}) %all-to-all-start) | async-done | bytes 2097184 | tf_op jit(solution)/shard_map/all_to_all | solution.py:26
  73.2 0.6 copy.81
  73.8 2.7 copy.63
  76.5 34.0 %all-gather.2.cloned.1.call-done = bf16[128,128,128]{2,1,0:T(8,128)(2,1)} async-done(((bf16[4,128,128]{2,1,0:T(8,128)(2,1)}), bf16[128,128,128]{2,1,0:T(8,128)(2,1)}) %all-gather.2.cloned.1.call-update) | async-done | bytes 4194320 | tf_op jit(solution)/shard_map/all_gather | solution.py:66
  110.5 36.9 %while.22 = (s32[]{:T(128)}, f32[128,6,128]{2,1,0:T(8,128)S(1)}, s32[4,32]{1,0:T(4,128)S(1)}, bf16[4,32,128,128]{3,2,1,0:T(8,128)(2,1)}, s32[4,32]{1,0:T(4,128)S...) while((s32[]{:T(128)}, f32[128,6,128]{2,1,0:T(8,128)S(1)}, s32[4,32]{1,0:T(4,128)S(1)}, ...), condition=%wide.region_3.5_spmd.clone, body=%wide.region_2.4_spmd.clone.sunk | while | flops 172688768 | bytes 13374515 | solution.py:83
  110.5 2.3 gather_fusion.2
  112.9 3.5 %convolution_bitcast_fusion.3 = f32[128,32,128]{0,2,1:T(8,128)} fusion(bf16[32,128,128]{2,1,0:T(8,128)(2,1)S(1)} %gather_fusion.2, bf16[4,32,128,128]{3,2,1,0:T(8,128)(2,1)} %get-tuple-element.304, s32[]{:T(128)S(6)} %copy.96, pred[32]{0:T(512)(128)(4,1)S(1)} %get-tuple-element.284), kind=kOutput, calls=%fused_computation.27.clone.1 | convolution fusion | flops 134742016 | bytes 4194340 | tf_op jit(solution)/shard_map/while/body/eval_jaxpr/rsj,sij->rsi/dot_general | solution.py:75
  116.4 2.4 copy.92
  118.7 0.9 fusion.71
  119.8 2.3 gather_fusion.2
  122.1 3.5 %convolution_bitcast_fusion.3 = f32[128,32,128]{0,2,1:T(8,128)} fusion(bf16[32,128,128]{2,1,0:T(8,128)(2,1)S(1)} %gather_fusion.2, bf16[4,32,128,128]{3,2,1,0:T(8,128)(2,1)} %get-tuple-element.304, s32[]{:T(128)S(6)} %copy.96, pred[32]{0:T(512)(128)(4,1)S(1)} %get-tuple-element.284), kind=kOutput, calls=%fused_computation.27.clone.1 | convolution fusion | flops 134742016 | bytes 4194340 | tf_op jit(solution)/shard_map/while/body/eval_jaxpr/rsj,sij->rsi/dot_general | solution.py:75
  125.6 2.4 copy.92
  128.0 0.9 fusion.71
  129.0 2.3 gather_fusion.2
  131.3 3.5 %convolution_bitcast_fusion.3 = f32[128,32,128]{0,2,1:T(8,128)} fusion(bf16[32,128,128]{2,1,0:T(8,128)(2,1)S(1)} %gather_fusion.2, bf16[4,32,128,128]{3,2,1,0:T(8,128)(2,1)} %get-tuple-element.304, s32[]{:T(128)S(6)} %copy.96, pred[32]{0:T(512)(128)(4,1)S(1)} %get-tuple-element.284), kind=kOutput, calls=%fused_computation.27.clone.1 | convolution fusion | flops 134742016 | bytes 4194340 | tf_op jit(solution)/shard_map/while/body/eval_jaxpr/rsj,sij->rsi/dot_general | solution.py:75
  134.8 2.4 copy.92
  137.2 0.9 fusion.71
  138.2 2.3 gather_fusion.2
  140.6 3.5 %convolution_bitcast_fusion.3 = f32[128,32,128]{0,2,1:T(8,128)} fusion(bf16[32,128,128]{2,1,0:T(8,128)(2,1)S(1)} %gather_fusion.2, bf16[4,32,128,128]{3,2,1,0:T(8,128)(2,1)} %get-tuple-element.304, s32[]{:T(128)S(6)} %copy.96, pred[32]{0:T(512)(128)(4,1)S(1)} %get-tuple-element.284), kind=kOutput, calls=%fused_computation.27.clone.1 | convolution fusion | flops 134742016 | bytes 4194340 | tf_op jit(solution)/shard_map/while/body/eval_jaxpr/rsj,sij->rsi/dot_general | solution.py:75
  144.1 2.4 copy.92
  146.4 0.9 fusion.71
  147.6 0.3 fusion.39
  148.0 19.4 %while.21 = (s32[]{:T(128)}, bf16[4,32,128,128]{3,2,1,0:T(8,128)(2,1)}, s32[4,32]{1,0:T(4,128)S(1)}, bf16[128,6,128]{2,0,1:T(8,128)(2,1)S(1)}, s32[4,32]{1,0:T(4...) while((s32[]{:T(128)}, bf16[4,32,128,128]{3,2,1,0:T(8,128)(2,1)}, ...), condition=%wide.region_6.8_spmd, body=%wide.region_5.7_spmd.sunk | while | flops 135793152 | bytes 8398573 | solution.py:109
  148.1 0.7 gather_fusion.1
  148.9 2.3 gather_fusion
  151.2 1.6 bitcast_dynamic-update-slice_fusion.2
  152.9 0.7 gather_fusion.1
  153.7 2.3 gather_fusion
  156.0 1.7 bitcast_dynamic-update-slice_fusion.2
  157.8 0.7 gather_fusion.1
  158.5 2.3 gather_fusion
  160.9 1.7 bitcast_dynamic-update-slice_fusion.2
  162.6 0.7 gather_fusion.1
  163.4 2.3 gather_fusion
  165.7 1.7 bitcast_dynamic-update-slice_fusion.2
  167.6 0.8 copy.74
  168.5 0.8 copy.73
  169.3 133.2 %reduce-scatter.2.cloned.1.call-done = bf16[4,128,128]{2,1,0:T(8,128)(2,1)} async-done(((bf16[128,128,128]{2,1,0:T(8,128)(2,1)}), bf16[4,128,128]{2,1,0:T(8,128)(2,1)}) %reduce-scatter.2.cloned.1.call-update) | async-done | bytes 131088 | tf_op jit(solution)/shard_map/reduce_scatter | solution.py:108
  302.5 1.5 fusion.28
  304.0 0.4 copy.72
  304.4 0.8 copy.90
  (69 shorter events, 2.1 us)
Async XLA Ops:
  7.2 4.1 %copy-start.2 = (bf16[8,8192]{1,0:T(8,128)(2,1)S(1)}, bf16[8,8192]{1,0:T(8,128)(2,1)}, u32[]{:S(2)}) copy-start(bf16[8,8192]{1,0:T(8,128)(2,1)} %param.12) | copy-start | bytes 393220
  7.2 103.3 %all-gather.2.cloned.1.call-start = ((), (), s32[]{:S(2)}) async-start(), calls=%async_computation.2 | async-start | bytes 4325376 | tf_op jit(solution)/shard_map/all_gather | solution.py:66
  12.9 13.1 %copy-start = (bf16[128,768]{1,0:T(8,128)(2,1)S(1)}, bf16[128,768]{1,0:T(8,128)(2,1)}, u32[]{:S(2)}) copy-start(bf16[128,768]{1,0:T(8,128)(2,1)} %param.14) | copy-start | bytes 589828
  12.9 13.2 %copy-start.1 = (bf16[128,768]{1,0:T(8,128)(2,1)S(1)}, bf16[128,768]{1,0:T(8,128)(2,1)}, u32[]{:S(2)}) copy-start(bf16[128,768]{1,0:T(8,128)(2,1)} %param.15) | copy-start | bytes 589828
  12.9 60.2 %all-to-all-start = ((bf16[16,8,8192]{2,1,0:T(8,128)(2,1)}), bf16[16,8,8192]{2,1,0:T(8,128)(2,1)S(1)}, u32[]{:S(2)}, u32[]{:S(2)}) async-start(bf16[16,8,8192]{2,1,0:T(8,128)(2,1)} %stack.2), calls=%async_computation | async-start | bytes 4194304 | tf_op jit(solution)/shard_map/all_to_all | solution.py:26
  24.4 278.1 %reduce-scatter.2.cloned.1.call-start = ((), (), s32[]{:S(2)}) async-start(), calls=%async_computation.3 | async-start | bytes 4325376 | tf_op jit(solution)/shard_map/reduce_scatter | solution.py:108
Sparse Core Ops, SparseCore 0:
  11.9 98.5 all-gather.1
  167.6 134.8 reduce-scatter.1
